TPU v7x, 32 devices: a whole 2x2x4 slice. The times are simulated.
32 devices in a mesh: rot: 8 (over y, x, core), az: 4 (over z).
Axes of the slice: x: 2, y: 2, z: 4, core: 2. Of those that a mesh axis runs over, the one named last changes fastest.
Arguments:
- inputs: bfloat16 [16, 4, 128, 128], P('rot', None, 'az'), may hold values from -6 to 6
- pre_one: bfloat16 [16, 4, 128, 128], P('rot', None, 'az'), may hold values from -8 to 8
- pre_two: bfloat16 [16, 4, 128, 128], P('rot', None, 'az'), may hold values from -8 to 8
- cotangent: bfloat16 [16, 4, 128, 128], P('rot', None, 'az'), may hold values from -6 to 6
- filt_one: bfloat16 [16, 3, 3, 128, 128], P('rot'), may hold values from -0.046875 to 0.046875
- filt_two: bfloat16 [16, 3, 3, 128, 128], P('rot'), may hold values from -0.046875 to 0.046875
Outputs:
- input_grad: bfloat16 [16, 4, 128, 128], P('rot', None, 'az')
- filt_grad_one: float32 [16, 3, 3, 128, 128], P('rot')
- filt_grad_two: float32 [16, 3, 3, 128, 128], P('rot')
All inputs are finite; a program needn't handle non-finite values.
Results may differ from a plain program's by a relative error of at most 0.018.
Values may be sent and summed in bfloat16 or wider, within the bound.
A program may use at most 64 MiB of HBM per device.

v0:
```python
import jax
import jax.numpy as jnp
from jax import lax
from jax.sharding import PartitionSpec as P


def with_halo(block, sides, width):
    for axis, dim in sides:
        count = lax.axis_size(axis)
        forward = [(i, i + 1) for i in range(count - 1)]
        forward.append((count - 1, 0))
        backward = [(target, source) for source, target in forward]
        low = lax.ppermute(
            lax.slice_in_dim(block, block.shape[dim] - width, None, axis=dim), axis, forward
        )
        high = lax.ppermute(lax.slice_in_dim(block, 0, width, axis=dim), axis, backward)
        block = jnp.concatenate([low, block, high], axis=dim)
    return block


def slope(pre):
    widened = pre.astype(jnp.float32)
    logistic = jax.nn.sigmoid(widened)
    return logistic * (1.0 + widened * (1.0 - logistic))


def pad_rows(field):
    return jnp.pad(field, ((0, 0), (1, 1), (0, 0), (0, 0)))


def doubled_rows(field):
    padded = pad_rows(field)
    return jnp.concatenate([padded, padded], axis=0)


def filter_terms(features, gradient, my_rank, per_dev):
    doubled = doubled_rows(features)
    orient_count = gradient.shape[0]
    row_count = gradient.shape[1]
    col_count = gradient.shape[2]
    channels = gradient.shape[3]
    results = []
    for slot_index in range(per_dev):
        shifted = lax.dynamic_slice_in_dim(doubled, my_rank * per_dev + slot_index, orient_count, 0)
        pieces = []
        for row_tap in range(3):
            for col_tap in range(3):
                window = shifted[:, row_tap : row_tap + row_count, col_tap : col_tap + col_count, :]
                pieces.append(
                    lax.dot_general(
                        window,
                        gradient,
                        (((0, 1, 2), (0, 1, 2)), ((), ())),
                        preferred_element_type=jnp.float32,
                    )
                )
        results.append(jnp.stack(pieces).reshape(3, 3, channels, channels))
    return jnp.stack(results)


def make_terms(doubled, my_rank, filt_local, row_count, col_count, first_row, row_span):
    orient_count = doubled.shape[0] // 2
    channels = doubled.shape[3]
    per_dev = filt_local.shape[0]
    summed = jnp.zeros((row_span, row_count, col_count, channels), jnp.float32)
    for slot_index in range(per_dev):
        relative = my_rank * per_dev + slot_index
        offset = (first_row - relative) % orient_count
        chosen = lax.dynamic_slice_in_dim(doubled, offset, row_span, 0)
        for row_tap in range(3):
            for col_tap in range(3):
                window = chosen[
                    :,
                    2 - row_tap : 2 - row_tap + row_count,
                    2 - col_tap : 2 - col_tap + col_count,
                    :,
                ]
                summed = summed + lax.dot_general(
                    window,
                    filt_local[slot_index, row_tap, col_tap],
                    (((3,), (1,)), ((), ())),
                    preferred_element_type=jnp.float32,
                )
    return summed


def shards(inputs, pre_one, pre_two, cotangent, filt_one, filt_two):
    per_dev = inputs.shape[0]
    row_count = inputs.shape[1]
    col_count = inputs.shape[2]
    my_rank = lax.axis_index("rot")
    cell_count = per_dev * lax.axis_size("rot") * row_count * col_count * lax.axis_size("az")
    norm_scale = cell_count ** (-0.5)
    act_one = jax.nn.silu(pre_one.astype(jnp.float32)).astype(jnp.bfloat16)
    grad_two = (cotangent.astype(jnp.float32) * slope(pre_two)).astype(jnp.bfloat16)
    stacked = jnp.concatenate([inputs, act_one, grad_two], axis=0)
    widened = with_halo(stacked, (("az", 2),), 1)
    inputs_rim = widened[0:per_dev]
    act_rim = widened[per_dev : 2 * per_dev]
    grad_rim = widened[2 * per_dev : 3 * per_dev]
    all_inputs, all_act, all_grad = (
        lax.all_gather(inputs_rim, "rot", axis=0, tiled=True),
        lax.all_gather(act_rim, "rot", axis=0, tiled=True),
        lax.all_gather(grad_rim, "rot", axis=0, tiled=True),
    )
    out_cols = all_grad.shape[2] - 2
    margin = (all_grad.shape[2] - col_count) // 2
    doubled_two = doubled_rows(all_grad)
    delta_one = lax.psum_scatter(
        make_terms(
            doubled_two,
            my_rank,
            filt_two,
            row_count,
            out_cols,
            jnp.int32(0),
            per_dev * lax.axis_size("rot"),
        ),
        "rot",
        scatter_dimension=0,
        tiled=True,
    )
    grad_inner = all_grad[:, :, margin : margin + col_count]
    filt_part_two = filter_terms(all_act, grad_inner, my_rank, per_dev)
    grad_one = (delta_one * slope(pre_one)).astype(jnp.bfloat16)
    grad_one_rim = with_halo(grad_one, (("az", 2),), 1)
    all_grad_one = lax.all_gather(grad_one_rim, "rot", axis=0, tiled=True)
    doubled_one = doubled_rows(all_grad_one)
    input_sum = lax.psum_scatter(
        make_terms(
            doubled_one,
            my_rank,
            filt_one,
            row_count,
            col_count,
            jnp.int32(0),
            lax.axis_size("rot") * per_dev,
        ).astype(jnp.bfloat16),
        "rot",
        scatter_dimension=0,
        tiled=True,
    )
    filt_part_one = filter_terms(all_inputs, all_grad_one[:, :, 1:-1], my_rank, per_dev)
    summed_one, summed_two = (
        lax.psum(filt_part_one.astype(jnp.bfloat16), "az").astype(jnp.float32),
        lax.psum(filt_part_two.astype(jnp.bfloat16), "az").astype(jnp.float32),
    )
    return (input_sum, summed_one * norm_scale, summed_two * norm_scale)


def solution(mesh):
    return jax.shard_map(
        shards,
        mesh=mesh,
        in_specs=(
            P("rot", None, "az", None),
            P("rot", None, "az", None),
            P("rot", None, "az", None),
            P("rot", None, "az", None),
            P("rot", None, None, None, None),
            P("rot", None, None, None, None),
        ),
        out_specs=(
            P("rot", None, "az", None),
            P("rot", None, None, None, None),
            P("rot", None, None, None, None),
        ),
        check_vma=False,
    )
```

profile of v0, /device:TPU:0, one launch (start us, length us, event | category | flops | bytes accessed | tf_op | source)
XLA Modules:
  0.0 203.7 jit_solution(10225011640854622660)
XLA Ops:
  7.2 1.0 fusion.197
  9.0 5.1 %collective-permute-start.1 = (bf16[6,4,1,128]{3,2,1,0:T(2,128)(2,1)S(1)}, bf16[6,4,1,128]{3,2,1,0:T(2,128)(2,1)S(1)}, u32[]{:S(2)}, u32[]{:S(2)}) collective-permute-start(bf16[6,4,1,128]{3,2,1,0:T(2,128)(2,1)S(1)} %get-tuple-element.17), channel_id=1, source_target_pairs={{1,0},{2,1},{3,2},{0,3},{5,4},{6,5},{7,6},{4,7},{9,8},{10,9},{11,1... | collective-permute-start | bytes 18440 | tf_op jit(solution)/shard_map/ppermute | solution.py:16
  14.1 1.4 collective-permute-done.1
  15.5 4.1 %collective-permute-done = bf16[6,4,1,128]{3,2,1,0:T(2,128)(2,1)S(1)} collective-permute-done((bf16[6,4,1,128]{3,2,1,0:T(2,128)(2,1)S(1)}, bf16[6,4,1,128]{3,2,1,0:T(2,128)(2,1)S(1)}, u32[]{:S(2)}, u32[]{:S(2)}) %collective-permute-start) | collective-permute-done | bytes 6176 | tf_op jit(solution)/shard_map/ppermute | solution.py:13
  19.6 1.0 pad_maximum_fusion.2
  20.6 10.0 %all_gather.12 = bf16[16,4,34,128]{3,1,2,0:T(4,128)(2,1)S(1)} all-gather(bf16[2,4,34,128]{3,1,2,0:T(4,128)(2,1)S(1)} %copy.9), channel_id=1, replica_groups=mesh['rot'=8,'az'=4] {'rot'}, dimensions={0}, use_global_device_ids=true | all-gather | bytes 626688 | tf_op jit(solution)/shard_map/all_gather | solution.py:104
  37.3 1.3 convolution_add_fusion.17
  38.7 10.0 %all_gather.14 = bf16[16,4,34,128]{3,1,2,0:T(4,128)(2,1)S(1)} all-gather(bf16[2,4,34,128]{3,1,2,0:T(4,128)(2,1)S(1)} %copy.13), channel_id=1, replica_groups=mesh['rot'=8,'az'=4] {'rot'}, dimensions={0}, use_global_device_ids=true | all-gather | bytes 626688 | tf_op jit(solution)/shard_map/all_gather | solution.py:102
  48.9 9.2 %all_gather.15 = bf16[16,4,34,128]{3,1,2,0:T(4,128)(2,1)S(1)} all-gather(bf16[2,4,34,128]{3,1,2,0:T(4,128)(2,1)S(1)} %copy.16), channel_id=1, replica_groups=mesh['rot'=8,'az'=4] {'rot'}, dimensions={0}, use_global_device_ids=true | all-gather | bytes 626688 | tf_op jit(solution)/shard_map/all_gather | solution.py:103
  64.0 1.7 fusion.112
  68.1 3.8 %reduce-scatter.3.cloned.1.call-done = f32[2,4,32,128]{3,2,1,0:T(8,128)} async-done(((f32[16,4,32,128]{3,2,1,0:T(8,128)}), f32[2,4,32,128]{3,2,1,0:T(8,128)}) %reduce-scatter.3.cloned.1.call-update) | async-done | bytes 131088 | tf_op jit(solution)/shard_map/reduce_scatter | solution.py:109
  72.0 1.0 fusion.205
  73.0 3.4 %collective-permute-start.3 = (bf16[2,4,1,128]{3,2,1,0:T(2,128)(2,1)S(1)}, bf16[2,4,1,128]{3,2,1,0:T(2,128)(2,1)S(1)}, u32[]{:S(2)}, u32[]{:S(2)}) collective-permute-start(bf16[2,4,1,128]{3,2,1,0:T(2,128)(2,1)S(1)} %get-tuple-element.19), channel_id=1, source_target_pairs={{1,0},{2,1},{3,2},{0,3},{5,4},{6,5},{7,6},{4,7},{9,8},{10,9},{11,1... | collective-permute-start | bytes 6152 | tf_op jit(solution)/shard_map/ppermute | solution.py:16
  77.7 4.1 %collective-permute-done.2 = bf16[2,4,1,128]{3,2,1,0:T(2,128)(2,1)S(1)} collective-permute-done((bf16[2,4,1,128]{3,2,1,0:T(2,128)(2,1)S(1)}, bf16[2,4,1,128]{3,2,1,0:T(2,128)(2,1)S(1)}, u32[]{:S(2)}, u32[]{:S(2)}) %collective-permute-start.2) | collective-permute-done | bytes 2080 | tf_op jit(solution)/shard_map/ppermute | solution.py:13
  81.8 10.2 %all_gather.13 = bf16[16,4,34,128]{3,1,2,0:T(4,128)(2,1)S(1)} all-gather(bf16[2,4,34,128]{3,1,2,0:T(4,128)(2,1)S(1)} %copy.11), channel_id=1, replica_groups=mesh['rot'=8,'az'=4] {'rot'}, dimensions={0}, use_global_device_ids=true | all-gather | bytes 626688 | tf_op jit(solution)/shard_map/all_gather | solution.py:127
  106.6 1.1 convolution_add_fusion.4
  107.7 1.1 convolution_add_fusion.3
  108.7 1.1 convolution_add_fusion.2
  109.8 1.1 convolution_add_fusion.1
  110.9 1.9 fusion
  112.8 47.2 %all-reduce.7.cloned.1.call-done = (bf16[2,3,3,128,128]{4,3,2,1,0:T(8,128)(2,1)}, bf16[2,3,3,128,128]{4,3,2,1,0:T(8,128)(2,1)}) async-done(((bf16[2,3,3,128,128]{4,3,2,1,0:T(8,128)(2,1)}, bf16[2,3,3,128,128]{4,3,2,1,0:T(8,128)(2,1)}), (bf16[2,3,3,128,128]{4,3,2,1,0:T(8,128)(2,1)}, bf16[2,3,3,128,128]{4,3,2,1,0:T(8,128)(2,1)})) %all-reduce.7.cloned.1.call-update) | async-done | bytes 1179664 | tf_op jit(solution)/shard_map/psum | solution.py:145
  159.9 2.3 %convert_multiply_fusion.1 = f32[2,3,3,128,128]{4,3,2,1,0:T(8,128)} fusion(bf16[2,3,3,128,128]{4,3,2,1,0:T(8,128)(2,1)} %get-tuple-element.3), kind=kLoop, calls=%fused_computation.52 | loop fusion | flops 589824 | bytes 1769472 | tf_op jit(solution)/shard_map/mul | solution.py:148
  162.2 1.2 convert_multiply_fusion
  163.4 33.8 %reduce-scatter.5.cloned.1.call-done = bf16[2,4,32,128]{3,2,1,0:T(8,128)(2,1)} async-done(((bf16[16,4,32,128]{3,2,1,0:T(8,128)(2,1)}), bf16[2,4,32,128]{3,2,1,0:T(8,128)(2,1)}) %reduce-scatter.5.cloned.1.call-update) | async-done | bytes 65552 | tf_op jit(solution)/shard_map/reduce_scatter | solution.py:129
  (106 shorter events, 31.9 us)
Async XLA Ops:
  7.2 64.8 %reduce-scatter.3.cloned.1.call-start = ((), (), s32[]{:S(2)}) async-start(), calls=%async_computation.2 | async-start | bytes 1179648 | tf_op jit(solution)/shard_map/reduce_scatter | solution.py:109
  9.0 6.5 %collective-permute-start.1 = (bf16[6,4,1,128]{3,2,1,0:T(2,128)(2,1)S(1)}, bf16[6,4,1,128]{3,2,1,0:T(2,128)(2,1)S(1)}, u32[]{:S(2)}, u32[]{:S(2)}) collective-permute-start(bf16[6,4,1,128]{3,2,1,0:T(2,128)(2,1)S(1)} %get-tuple-element.17), channel_id=1, source_target_pairs={{1,0},{2,1},{3,2},{0,3},{5,4},{6,5},{7,6},{4,7},{9,8},{10,9},{11,1... | collective-permute-start | bytes 18440 | tf_op jit(solution)/shard_map/ppermute | solution.py:16
  14.1 5.5 %collective-permute-start = (bf16[6,4,1,128]{3,2,1,0:T(2,128)(2,1)S(1)}, bf16[6,4,1,128]{3,2,1,0:T(2,128)(2,1)S(1)}, u32[]{:S(2)}, u32[]{:S(2)}) collective-permute-start(bf16[6,4,1,128]{3,2,1,0:T(2,128)(2,1)S(1)} %get-tuple-element.16), channel_id=1, source_target_pairs={{0,1},{1,2},{2,3},{3,0},{4,5},{5,6},{6,7},{7,4},{8,9},{9,10},{10,1... | collective-permute-start | bytes 18440 | tf_op jit(solution)/shard_map/ppermute | solution.py:13
  30.8 1.1 copy-start.3
  38.6 121.4 %all-reduce.7.cloned.1.call-start = ((), (), s32[]{:S(2)}) async-start(), calls=%async_computation.4 | async-start | bytes 2359296 | tf_op jit(solution)/shard_map/psum | solution.py:145
  67.7 4.3 %copy-start.4 = (bf16[2,4,32,128]{3,2,1,0:T(8,128)(2,1)S(1)}, bf16[2,4,32,128]{3,2,1,0:T(8,128)(2,1)}, u32[]{:S(2)}) copy-start(bf16[2,4,32,128]{3,2,1,0:T(8,128)(2,1)} %param.7) | copy-start | bytes 196612
  73.0 4.7 %collective-permute-start.3 = (bf16[2,4,1,128]{3,2,1,0:T(2,128)(2,1)S(1)}, bf16[2,4,1,128]{3,2,1,0:T(2,128)(2,1)S(1)}, u32[]{:S(2)}, u32[]{:S(2)}) collective-permute-start(bf16[2,4,1,128]{3,2,1,0:T(2,128)(2,1)S(1)} %get-tuple-element.19), channel_id=1, source_target_pairs={{1,0},{2,1},{3,2},{0,3},{5,4},{6,5},{7,6},{4,7},{9,8},{10,9},{11,1... | collective-permute-start | bytes 6152 | tf_op jit(solution)/shard_map/ppermute | solution.py:16
  76.3 5.4 %collective-permute-start.2 = (bf16[2,4,1,128]{3,2,1,0:T(2,128)(2,1)S(1)}, bf16[2,4,1,128]{3,2,1,0:T(2,128)(2,1)S(1)}, u32[]{:S(2)}, u32[]{:S(2)}) collective-permute-start(bf16[2,4,1,128]{3,2,1,0:T(2,128)(2,1)S(1)} %get-tuple-element.18), channel_id=1, source_target_pairs={{0,1},{1,2},{2,3},{3,0},{4,5},{5,6},{6,7},{7,4},{8,9},{9,10},{10,1... | collective-permute-start | bytes 6152 | tf_op jit(solution)/shard_map/ppermute | solution.py:13
  92.2 1.1 copy-start.2
  97.0 1.2 copy-start
  106.5 90.6 %reduce-scatter.5.cloned.1.call-start = ((), (), s32[]{:S(2)}) async-start(), calls=%async_computation.3 | async-start | bytes 589824 | tf_op jit(solution)/shard_map/reduce_scatter | solution.py:129
  159.9 2.3 %copy-start.1 = (bf16[2,3,3,128,128]{4,3,2,1,0:T(8,128)(2,1)S(1)}, bf16[2,3,3,128,128]{4,3,2,1,0:T(8,128)(2,1)}, u32[]{:S(2)}) copy-start(bf16[2,3,3,128,128]{4,3,2,1,0:T(8,128)(2,1)} %get-tuple-element.4) | copy-start | bytes 1769476
Sparse Core Ops, SparseCore 0:
  38.7 33.2 reduce-scatter.2
  106.6 53.2 all-reduce.6
  163.6 33.5 reduce-scatter.4
where the time goes:
time: 205 us; the launch traced here: 204 us
  waiting for transfers between devices  94.8 us (46%)
  blocking collectives  39.3 us (19%)
  matrix products  31.5 us (15%)
  between operations  14.1 us (7%)
  other arithmetic  13 us (6%)
  starting transfers between devices  8.63 us (4%)
  local copies, waits for them, and re-layouts  2.34 us (1%)
    psum x1, waiting for transfers between devices, shards(): lax.psum(filt_part_one.astype(jnp.bfloat16), 'az').astype(jnp.float32)  47.2 us
    reduce_scatter x1, waiting for transfers between devices, shards(): lax.psum_scatter(make_terms(doubled_one, my_rank, filt_one, row_count, co...  33.8 us
    dot_general x36, matrix products, make_terms(): lax.dot_general(window, filt_local[slot_index, row_tap, col_tap], (((3,),...  16.8 us
    dot_general x36, matrix products, filter_terms(): lax.dot_general(window, gradient, (((0, 1, 2), (0, 1, 2)), ((), ())), pre...  14.7 us
    all_gather x1, blocking collectives, shards(): all_grad_one = lax.all_gather(grad_one_rim, 'rot', axis=0, tiled=True)  10.2 us
    all_gather x1, blocking collectives, shards(): lax.all_gather(grad_rim, 'rot', axis=0, tiled=True)  9.99 us
    all_gather x1, blocking collectives, shards(): lax.all_gather(inputs_rim, 'rot', axis=0, tiled=True)  9.96 us
    all_gather x1, blocking collectives, shards(): lax.all_gather(act_rim, 'rot', axis=0, tiled=True)  9.19 us
  transfers between devices with their start and end apart: 7, of which 7 were waited for; matrix products, arithmetic and copies ran while one was open for 10% of the time, Pallas kernels for 0%

commit v1 on v0

v1 whole, which is shorter than its diff:
```python
import functools

import jax
import jax.numpy as jnp
from jax import lax
from jax.experimental import pallas as pl
from jax.experimental.pallas import tpu as pltpu
from jax.sharding import PartitionSpec as P

F32 = jnp.float32
BF16 = jnp.bfloat16


def slope(v):
    s = jax.nn.sigmoid(v)
    return s * (1.0 + v * (1.0 - s))


def kernel(
    n, m, p, H, X, C, scale,
    inputs, pre_one, pre_two, cot, filt_one, filt_two,
    out_in, out_f1, out_f2,
    st_g, st_e, st_a, grads, edges, feats, weights, gx, lhs, outs,
    part_s, part_r, zs, zr, zt, za,
    g_ss, g_rs, e_ss, e_rs, a_ss, a_rs, p_ss, p_rs, z_ss, z_rs, y_ss, y_rs,
):
    R = n * p
    HX = H * X
    me = lax.axis_index("rot")
    z = lax.axis_index("az")

    def rank(q):
        return lax.rem(me + q, n)

    def col(d):
        return lax.rem(z + d, m)

    def copy(src, dst, ss, rs, rot, az):
        return pltpu.make_async_remote_copy(
            src_ref=src, dst_ref=dst, send_sem=ss, recv_sem=rs,
            device_id={"rot": rot, "az": az}, device_id_type=pl.DeviceIdType.MESH,
        )

    barrier = pltpu.get_barrier_semaphore()
    near = sorted({0, 1 % m, (m - 1) % m})
    partners = [(q, d) for d in near for q in range(n)]
    partners += [(0, d) for d in range(m) if d not in near]
    partners = [pair for pair in partners if pair != (0, 0)]
    for q, d in partners:
        pl.semaphore_signal(
            barrier, inc=1, device_id={"rot": rank(q), "az": col(d)},
            device_id_type=pl.DeviceIdType.MESH,
        )

    pending = []

    def start(c):
        c.start()
        pending.append(c)
        return c

    def stage_grad(ph, value):
        st_g[ph] = value.astype(BF16)
        grads[ph, me] = value.astype(BF16)
        st_e[ph, 0] = value[:, :, 0, :].reshape(p * H, C)
        st_e[ph, 1] = value[:, :, X - 1, :].reshape(p * H, C)

    def send_grad(ph):
        g_copies = [
            start(copy(st_g.at[ph], grads.at[ph, me], g_ss.at[ph, q], g_rs.at[ph, q], rank(q), z))
            for q in range(1, n)
        ]
        for q in range(n):
            for side, d in ((1, 1), (0, m - 1)):
                g_copies.append(
                    start(
                        copy(
                            st_e.at[ph, side], edges.at[ph, 1 - side, me],
                            e_ss.at[ph, side, q], e_rs.at[ph, side, q], rank(q), col(d),
                        )
                    )
                )
        return g_copies

    def stage_feat(ph, value):
        for o in range(p):
            turned = value[o].T.astype(BF16)
            st_a[ph, o] = turned
            feats[ph, 0, o] = turned

    def send_feat(ph):
        return [
            start(copy(st_a.at[ph], feats.at[ph, n - q], a_ss.at[ph, q], a_rs.at[ph, q], rank(q), z))
            for q in range(1, n)
        ]

    def build_gx(ph):
        x_of = lax.broadcasted_iota(jnp.int32, (p * H, X, C), 1).reshape(p * HX, C)

        def body(d, carry):
            g = grads[ph, d].astype(F32).reshape(p * HX, C)
            low = jnp.broadcast_to(edges[ph, 0, d][:, None, :], (p * H, X, C)).reshape(p * HX, C)
            high = jnp.broadcast_to(edges[ph, 1, d][:, None, :], (p * H, X, C)).reshape(p * HX, C)
            before = jnp.where(x_of == 0, low, pltpu.roll(g, 1, 0))
            after = jnp.where(x_of == X - 1, high, pltpu.roll(g, p * HX - 1, 0))
            for j, v in enumerate((after, g, before)):
                gx[pl.ds(d * p, p), 1 : H + 1, :, j * C : (j + 1) * C] = v.astype(BF16).reshape(p, H, X, C)
            return carry

        lax.fori_loop(0, n, body, 0)

    def build_weights(filt):
        for s in range(p):
            for i in range(3):
                for j in range(3):
                    weights[s * C : (s + 1) * C, (i * 3 + j) * C : (i * 3 + j + 1) * C] = filt[s, i, j]

    def build_lhs(ph):
        lane = lax.broadcasted_iota(jnp.int32, (C, HX), 1)
        for q in range(n):
            for o in range(p):
                block = q * p + o
                a = feats[ph, q, o]
                wide = a.astype(F32)
                down = jnp.where(lane < X, 0.0, pltpu.roll(wide, X, 1)).astype(BF16)
                up = jnp.where(lane >= HX - X, 0.0, pltpu.roll(wide, HX - X, 1)).astype(BF16)
                spots = [block] + ([R + block] if block < p - 1 else [])
                for spot in spots:
                    for i, v in enumerate((down, a, up)):
                        lhs[i * C : (i + 1) * C, spot * HX : (spot + 1) * HX] = v

    def data_terms(ph):
        copies = []
        w = weights[...]

        def product(q):
            rows = jnp.concatenate(
                [gx[q * p : (q + 1) * p, 2 - i : 2 - i + H].reshape(p * HX, 3 * C) for i in range(3)],
                axis=1,
            )
            got = lax.dot_general(rows, w, (((1,), (1,)), ((), ())), preferred_element_type=F32)
            outs[q * p : (q + 1) * p] = got.reshape(p, HX, p * C)

        def emit(q):
            for o in range(p):
                total = None
                for s in range(p):
                    term = outs[(q * p + o - s) % R, :, s * C : (s + 1) * C]
                    total = term if total is None else total + term
                if q == 0:
                    part_r[ph, 0, o] = total.astype(BF16)
                else:
                    part_s[ph, q, o] = total.astype(BF16)
            if q > 0:
                copies.append(
                    start(
                        copy(part_s.at[ph, q], part_r.at[ph, q], p_ss.at[ph, q], p_rs.at[ph, q], rank(q), z)
                    )
                )

        for q in range(n):
            product(q)
            if q > 0:
                emit(q)
        emit(0)
        return copies

    def part_sum(ph, copies):
        for c in copies:
            c.wait_recv()
        total = part_r[ph, 0].astype(F32)
        for q in range(1, n):
            total = total + part_r[ph, q].astype(F32)
        return total

    K = p * 9
    cm = C // m

    def filt_terms(ph):
        right = gx[:, 1 : H + 1].reshape(R * HX, 3 * C)
        for s in range(p):
            got = jnp.dot(
                lhs[:, s * HX : (s + R) * HX], right, preferred_element_type=F32
            )
            for i in range(3):
                for j in range(3):
                    tile = got[i * C : (i + 1) * C, j * C : (j + 1) * C].astype(F32).reshape(m, cm, C)
                    zs[ph, :, s * 9 + i * 3 + j] = tile.astype(BF16)
        return [
            start(copy(zs.at[ph, col(d)], zr.at[ph, d], z_ss.at[ph, d], z_rs.at[ph, d], me, col(d)))
            for d in range(1, m)
        ]

    def filt_sum(ph, copies):
        for c in copies:
            c.wait_recv()
        total = zs[ph, z].astype(F32)
        for d in range(1, m):
            total = total + zr[ph, d].astype(F32)
        total = total.astype(BF16)
        zt[ph] = total
        za[ph, z] = total
        return [
            start(copy(zt.at[ph], za.at[ph, z], y_ss.at[ph, d], y_rs.at[ph, d], me, col(d)))
            for d in range(1, m)
        ]

    def filt_out(ph, copies, out):
        for c in copies:
            c.wait_recv()
        for c in range(m):
            out[:, :, :, c * cm : (c + 1) * cm, :] = (za[ph, c].astype(F32) * scale).reshape(p, 3, 3, cm, C)

    grad_two = (cot[...].astype(F32) * slope(pre_two[...].astype(F32))).astype(BF16).astype(F32)
    stage_grad(0, grad_two)
    wide_one = pre_one[...].astype(F32)
    stage_feat(0, (wide_one * jax.nn.sigmoid(wide_one)).reshape(p, HX, C))
    stage_feat(1, inputs[...].astype(F32).reshape(p, HX, C))
    pl.semaphore_wait(barrier, len(partners))

    g_copies = send_grad(0)
    a_copies = send_feat(0)
    i_copies = send_feat(1)
    build_weights(filt_two)
    gx[:, 0] = jnp.zeros((R, X, 3 * C), BF16)
    gx[:, H + 1] = jnp.zeros((R, X, 3 * C), BF16)
    for c in g_copies:
        c.wait_recv()
    build_gx(0)
    p_copies = data_terms(0)
    for c in a_copies:
        c.wait_recv()
    build_lhs(0)
    z_copies = filt_terms(0)

    delta = part_sum(0, p_copies).reshape(p, H, X, C)
    grad_one = (delta * slope(pre_one[...].astype(F32))).astype(BF16).astype(F32)
    stage_grad(1, grad_one)
    g_copies = send_grad(1)
    build_weights(filt_one)
    for c in i_copies:
        c.wait_recv()
    build_lhs(1)
    for c in g_copies:
        c.wait_recv()
    build_gx(1)
    p_copies = data_terms(1)
    w_copies = filt_terms(1)
    y_two = filt_sum(0, z_copies)
    out_in[...] = part_sum(1, p_copies).astype(BF16).reshape(p, H, X, C)
    y_one = filt_sum(1, w_copies)
    filt_out(0, y_two, out_f2)
    filt_out(1, y_one, out_f1)
    for c in pending:
        c.wait_send()


def solution(mesh):
    n, m = mesh.shape["rot"], mesh.shape["az"]

    def shards(inputs, pre_one, pre_two, cot, filt_one, filt_two):
        p, H, X, C = inputs.shape
        R, HX, K, cm = n * p, H * X, p * 9, C // m
        scale = float(R * H * X * m) ** -0.5
        dma = pltpu.SemaphoreType.DMA
        vmem = pl.BlockSpec(memory_space=pltpu.VMEM)
        filt = jax.ShapeDtypeStruct((p, 3, 3, C, C), F32)
        return pl.pallas_call(
            functools.partial(kernel, n, m, p, H, X, C, scale),
            out_shape=(jax.ShapeDtypeStruct((p, H, X, C), BF16), filt, filt),
            in_specs=[vmem] * 6,
            out_specs=(vmem,) * 3,
            scratch_shapes=[
                pltpu.VMEM((2, p, H, X, C), BF16),
                pltpu.VMEM((2, 2, p * H, C), F32),
                pltpu.VMEM((2, p, C, HX), BF16),
                pltpu.VMEM((2, n, p, H, X, C), BF16),
                pltpu.VMEM((2, 2, n, p * H, C), F32),
                pltpu.VMEM((2, n, p, C, HX), BF16),
                pltpu.VMEM((p * C, 9 * C), BF16),
                pltpu.VMEM((R, H + 2, X, 3 * C), BF16),
                pltpu.VMEM((3 * C, (R + p - 1) * HX), BF16),
                pltpu.VMEM((R, HX, p * C), F32),
                pltpu.VMEM((2, n, p, HX, C), BF16),
                pltpu.VMEM((2, n, p, HX, C), BF16),
                pltpu.VMEM((2, m, K, cm, C), BF16),
                pltpu.VMEM((2, m, K, cm, C), BF16),
                pltpu.VMEM((2, K, cm, C), BF16),
                pltpu.VMEM((2, m, K, cm, C), BF16),
                dma((2, n)), dma((2, n)),
                dma((2, 2, n)), dma((2, 2, n)),
                dma((2, n)), dma((2, n)),
                dma((2, n)), dma((2, n)),
                dma((2, m)), dma((2, m)),
                dma((2, m)), dma((2, m)),
            ],
            compiler_params=pltpu.CompilerParams(
                collective_id=0, has_side_effects=True, vmem_limit_bytes=60 * 1024 * 1024
            ),
        )(inputs, pre_one, pre_two, cot, filt_one, filt_two)

    cells = P("rot", None, "az", None)
    banks = P("rot", None, None, None, None)
    return jax.shard_map(
        shards, mesh=mesh,
        in_specs=(cells,) * 4 + (banks,) * 2,
        out_specs=(cells, banks, banks),
        check_vma=False,
    )
```

time: 205 us -> 93.2 us (0.45)
  waiting for transfers between devices: 94.8 us -> 0 us
  Pallas kernels: 0 us -> 86.4 us
  blocking collectives: 39.3 us -> 0 us
  matrix products: 31.5 us -> 0 us
  between operations: 14.1 us -> 0.64 us
  other arithmetic: 13 us -> 0 us
  starting transfers between devices: 8.63 us -> 0 us
  local copies, waits for them, and re-layouts: 2.34 us -> 4.97 us
    pallas_call x0 -> x1, Pallas kernels: none -> 86.4 us  [shards(): pl.pallas_call(functools.partial(kernel, n, m, p, H, X, C, scale), out_sh...]
    psum x1 -> x0, waiting for transfers between devices: 47.2 us -> none  [shards(): lax.psum(filt_part_one.astype(jnp.bfloat16), 'az').astype(jnp.float32)]
    all_gather x4 -> x0, blocking collectives: 39.3 us -> none  [the longest x1 10.2 us: shards(): all_grad_one = lax.all_gather(grad_one_rim, 'rot', axis=0, tiled=True)]
    reduce_scatter x2 -> x0, waiting for transfers between devices: 37.6 us -> none  [the longest x1 33.8 us: shards(): lax.psum_scatter(make_terms(doubled_one, my_rank, filt_one, row_count, co...]
    dot_general x72 -> x0, matrix products: 31.5 us -> none  [the longest x36 16.8 us: make_terms(): lax.dot_general(window, filt_local[slot_index, row_tap, col_tap], (((3,),...]
    ppermute x4 -> x0, waiting for transfers between devices: 10 us -> none  [the longest x2 8.16 us: with_halo(): lax.ppermute(lax.slice_in_dim(block, block.shape[dim] - width, None, axis...]
    ppermute x4 -> x0, starting transfers between devices: 8.51 us -> none  [the longest x2 8.5 us: with_halo(): lax.ppermute(lax.slice_in_dim(block, 0, width, axis=dim), axis, backward)]
    concatenate x6 -> x0, other arithmetic: 5.07 us -> none  [the longest x4 4.08 us: doubled_rows(): return jnp.concatenate([padded, padded], axis=0)]
  transfers between devices with their start and end apart: 7 -> 0, of which waited for: 7 -> 0; matrix products, arithmetic and copies ran while one was open for 10% -> 0% of each run, Pallas kernels for 0% -> 0%
where the time goes in v1:
time: 93.2 us; the launch traced here: 92 us
  Pallas kernels  86.4 us (93%)
  local copies, waits for them, and re-layouts  4.97 us (5%)
    pallas_call x1, Pallas kernels, shards(): pl.pallas_call(functools.partial(kernel, n, m, p, H, X, C, scale), out_sh...  86.4 us
    unnamed x5, local copies, waits for them, and re-layouts  4.97 us

profile of v1, /device:TPU:0, one launch (start us, length us, event | category | flops | bytes accessed | tf_op | source)
XLA Modules:
  0.0 92.0 jit_solution(9376487636319477350)
XLA Ops:
  0.6 86.4 %shard_map.85 = (bf16[2,4,32,128]{3,2,1,0:T(8,128)(2,1)}, f32[2,3,3,128,128]{4,3,2,1,0:T(8,128)}, f32[2,3,3,128,128]{4,3,2,1,0:T(8,128)}) custom-call(bf16[2,4,32,128]{3,2,1,0:T(8,128)(2,1)} %inputs.1, bf16[2,4,32,128]{3,2,1,0:T(8,128)(2,1)} %pre_one.1, bf16[2,4,32,128]{3,2,1,0:T(8,128)(2,1)} %pre_two.1, bf16[2,4,32,128]{3,2,1,0:T(8,128)(2,1)} %cot.1, ...), custom_call_target="tpu_custom_call" | custom-call | tf_op jit(solution)/shard_map/pallas_call | solution.py:268
  87.1 1.5 %copy.12 = bf16[2,4,32,128]{3,2,1,0:T(8,128)(2,1)} copy(bf16[2,4,32,128]{3,2,1,0:T(8,128)(2,1)} %get-tuple-element.6) | data formatting | bytes 131072
  88.5 0.0 copy-start
  88.5 2.5 %copy.13 = f32[2,3,3,128,128]{4,3,2,1,0:T(8,128)} copy(f32[2,3,3,128,128]{4,3,2,1,0:T(8,128)} %get-tuple-element.7) | data formatting | bytes 2359296
  91.0 0.0 copy-done
  91.0 1.0 %copy.14 = f32[2,3,3,128,128]{4,3,2,1,0:T(8,128)} copy(f32[2,3,3,128,128]{4,3,2,1,0:T(8,128)S(1)} %copy-done) | data formatting | bytes 2359296
Async XLA Ops:
  88.5 2.5 %copy-start = (f32[2,3,3,128,128]{4,3,2,1,0:T(8,128)S(1)}, f32[2,3,3,128,128]{4,3,2,1,0:T(8,128)}, u32[]{:S(2)}) copy-start(f32[2,3,3,128,128]{4,3,2,1,0:T(8,128)} %get-tuple-element.8) | copy-start | bytes 3538948

commit v2 on v1

v2 whole, which is shorter than its diff:
```python
import functools

import jax
import jax.numpy as jnp
from jax import lax
from jax.experimental import pallas as pl
from jax.experimental.pallas import tpu as pltpu
from jax.sharding import PartitionSpec as P

F32 = jnp.float32
BF16 = jnp.bfloat16


def slope(v):
    s = jax.nn.sigmoid(v)
    return s * (1.0 + v * (1.0 - s))


def kernel(
    n, m, p, H, X, C,
    inputs, pre_one, pre_two, cot, filt_one, filt_two,
    out_in, out_f1, out_f2,
    st_g, st_e, st_a, grads, edges, feats, weights, gx, lhs, outs,
    part_s, part_x, part_m, part_r, zs, zr, zt,
    g_ss, g_rs, gf_ss, gf_rs, e_ss, e_rs, ef_ss, ef_rs, a_ss, a_rs, af_ss, af_rs,
    x_ss, x_rs, p_ss, p_rs, z_ss, z_rs, y_ss, y_rs,
):
    R = n * p
    HX = H * X
    nc = n // 2
    half = C // 2
    K = 3 * p
    me = lax.axis_index("rot")
    z = lax.axis_index("az")
    core = lax.rem(me, 2)
    chip = lax.div(me, 2)
    sib = me + 1 - 2 * core

    def to(t):
        return 2 * lax.rem(chip + t, nc) + core

    def frm(t):
        return 2 * lax.rem(chip + nc - t, nc) + core

    def col(d):
        return lax.rem(z + d, m)

    def copy(src, dst, ss, rs, rot, az):
        return pltpu.make_async_remote_copy(
            src_ref=src, dst_ref=dst, send_sem=ss, recv_sem=rs,
            device_id={"rot": rot, "az": az}, device_id_type=pl.DeviceIdType.MESH,
        )

    barrier = pltpu.get_barrier_semaphore()
    near_cols = sorted({1 % m, (m - 1) % m})
    partners = [(sib, z)] + [(to(t), z) for t in range(1, nc)]
    partners += [(to(t), col(d)) for d in near_cols for t in range(nc)]
    for rot, az in partners:
        pl.semaphore_signal(
            barrier, inc=1, device_id={"rot": rot, "az": az},
            device_id_type=pl.DeviceIdType.MESH,
        )

    pending = []

    def start(c):
        c.start()
        pending.append(c)
        return c

    def stage_grad(ph, value):
        st_g[ph] = value.astype(BF16)
        grads[ph, me] = value.astype(BF16)
        st_e[ph, 0] = value[:, :, 0, :].reshape(p * H, C).astype(BF16)
        st_e[ph, 1] = value[:, :, X - 1, :].reshape(p * H, C).astype(BF16)

    def send_grad(ph):
        direct = [None] + [
            start(copy(st_g.at[ph], grads.at[ph, me], g_ss.at[ph, t], g_rs.at[ph, t], to(t), z))
            for t in range(1, nc)
        ]
        own = start(copy(st_g.at[ph], grads.at[ph, me], gf_ss.at[ph, 0], gf_rs.at[ph, 0], sib, z))
        rims = []
        for t in range(nc):
            for side, d in ((1, 1), (0, m - 1)):
                rims.append(
                    start(
                        copy(
                            st_e.at[ph, side], edges.at[ph, me, 1 - side],
                            e_ss.at[ph, side, t], e_rs.at[ph, side, t], to(t), col(d),
                        )
                    )
                )
        return direct, own, rims

    def relay_grad(ph, sent):
        direct, own, rims = sent
        passed = [own]
        for t in range(nc):
            rims[2 * t].wait_recv()
            rims[2 * t + 1].wait_recv()
            d = frm(t)
            passed.append(
                start(copy(edges.at[ph, d], edges.at[ph, d], ef_ss.at[ph, t], ef_rs.at[ph, t], sib, z))
            )
        for t in range(1, nc):
            direct[t].wait_recv()
            d = frm(t)
            passed.append(
                start(copy(grads.at[ph, d], grads.at[ph, d], gf_ss.at[ph, t], gf_rs.at[ph, t], sib, z))
            )
        return passed

    def stage_feat(ph, value):
        for o in range(p):
            turned = value[o].T.astype(BF16)
            st_a[ph, o] = turned
            feats[ph, me, o] = turned

    def send_feat(ph):
        direct = [None] + [
            start(copy(st_a.at[ph], feats.at[ph, me], a_ss.at[ph, t], a_rs.at[ph, t], to(t), z))
            for t in range(1, nc)
        ]
        own = start(copy(st_a.at[ph], feats.at[ph, me], af_ss.at[ph, 0], af_rs.at[ph, 0], sib, z))
        return direct, own

    def relay_feat(ph, sent):
        direct, own = sent
        passed = [own]
        for t in range(1, nc):
            direct[t].wait_recv()
            d = frm(t)
            passed.append(
                start(copy(feats.at[ph, d], feats.at[ph, d], af_ss.at[ph, t], af_rs.at[ph, t], sib, z))
            )
        return passed

    def arrive(copies):
        for c in copies:
            c.wait_recv()

    def build_gx(ph):
        x_of = lax.broadcasted_iota(jnp.int32, (p * H, X, C), 1).reshape(p * HX, C)

        def body(d, carry):
            g = grads[ph, d].astype(F32).reshape(p * HX, C)
            low = edges[ph, d, 0].astype(F32)
            high = edges[ph, d, 1].astype(F32)
            low = jnp.broadcast_to(low[:, None, :], (p * H, X, C)).reshape(p * HX, C)
            high = jnp.broadcast_to(high[:, None, :], (p * H, X, C)).reshape(p * HX, C)
            before = jnp.where(x_of == 0, low, pltpu.roll(g, 1, 0))
            after = jnp.where(x_of == X - 1, high, pltpu.roll(g, p * HX - 1, 0))
            for j, v in enumerate((after, g, before)):
                gx[pl.ds(d * p, p), 1 : H + 1, :, j * C : (j + 1) * C] = v.astype(BF16).reshape(p, H, X, C)
            return carry

        lax.fori_loop(0, n, body, 0)

    def build_weights(filt):
        for s in range(p):
            for i in range(3):
                for j in range(3):
                    weights[s * C : (s + 1) * C, (i * 3 + j) * C : (i * 3 + j + 1) * C] = filt[s, i, j]

    def build_lhs(ph):
        lane = lax.broadcasted_iota(jnp.int32, (C, HX), 1)
        for q in range(n):
            owner = lax.rem(me + q, n)
            for o in range(p):
                block = q * p + o
                a = feats[ph, owner, o]
                wide = a.astype(F32)
                down = jnp.where(lane < X, 0.0, pltpu.roll(wide, X, 1)).astype(BF16)
                up = jnp.where(lane >= HX - X, 0.0, pltpu.roll(wide, HX - X, 1)).astype(BF16)
                spots = [block] + ([R + block] if block < p - 1 else [])
                for spot in spots:
                    for i, v in enumerate((down, a, up)):
                        lhs[i * C : (i + 1) * C, spot * HX : (spot + 1) * HX] = v

    def term(q, o):
        total = None
        for s in range(p):
            one = outs[(q * p + o - s) % R, :, s * C : (s + 1) * C]
            total = one if total is None else total + one
        return total

    def data_terms(ph):
        w = weights[...]
        crossed = [None] * n

        def emit(q):
            for o in range(p):
                part_s[ph, q, o] = term(q, o).astype(BF16)
            t = lax.rem(q // 2 + core, nc)
            crossed[q] = start(
                copy(part_s.at[ph, q], part_x.at[ph, t], x_ss.at[ph, t], x_rs.at[ph, t], sib, z)
            )

        for q in range(n):
            rows = jnp.concatenate(
                [gx[q * p : (q + 1) * p, 2 - i : 2 - i + H].reshape(p * HX, 3 * C) for i in range(3)],
                axis=1,
            )
            got = lax.dot_general(rows, w, (((1,), (1,)), ((), ())), preferred_element_type=F32)
            outs[q * p : (q + 1) * p] = got.reshape(p, HX, p * C)
            if q % 2 == 1:
                emit(q)

    def merge_terms(ph):
        sent = []
        for t in list(range(1, nc)) + [0]:
            pltpu.make_async_remote_copy(
                src_ref=part_x.at[ph, t], dst_ref=part_x.at[ph, t],
                send_sem=x_ss.at[ph, t], recv_sem=x_rs.at[ph, t],
                device_id={"rot": sib, "az": z}, device_id_type=pl.DeviceIdType.MESH,
            ).wait_recv()
            for o in range(p):
                total = term(2 * t, o) + part_x[ph, t, o].astype(F32)
                if t == 0:
                    part_r[ph, 0, o] = total.astype(BF16)
                else:
                    part_m[ph, t, o] = total.astype(BF16)
            if t > 0:
                sent.append(
                    start(
                        copy(part_m.at[ph, t], part_r.at[ph, t], p_ss.at[ph, t], p_rs.at[ph, t], to(t), z)
                    )
                )
        return sent

    def part_sum(ph, copies):
        arrive(copies)
        total = part_r[ph, 0].astype(F32)
        for t in range(1, nc):
            total = total + part_r[ph, t].astype(F32)
        return total

    fg = (out_f2, out_f1)
    lower = z < m // 2
    near_pos = jnp.where(lower, z, m - 1 - z)
    near_h = jnp.where(lower, 0, 1)
    far_h = 1 - near_h
    right, left = jnp.minimum(z + 1, m - 1), jnp.maximum(z - 1, 0)
    inner = jnp.where(lower, right, left)
    outer = jnp.where(lower, left, right)
    at_end = near_pos == 0

    def final(ph, h, k):
        return fg[ph].at[k, :, pl.ds(pl.multiple_of(h * half, half), half), :]

    def hop(src, ph, h, k, az):
        return copy(src, zr.at[ph, h, k], z_ss.at[ph, h, k], z_rs.at[ph, h, k], me, az)

    def back(ph, h, k, az):
        return copy(final(ph, h, k), final(ph, h, k), y_ss.at[ph, h, k], y_rs.at[ph, h, k], me, az)

    def filt_terms(ph):
        right_side = gx[:, 1 : H + 1].reshape(R * HX, 3 * C)
        for s in range(p):
            got = jnp.dot(
                lhs[:, s * HX : (s + R) * HX], right_side, preferred_element_type=F32
            )
            for i in range(3):
                k = s * 3 + i
                for j in range(3):
                    tile = got[i * C : (i + 1) * C, j * C : (j + 1) * C]
                    zs[ph, :, k, j] = tile.reshape(2, half, C).astype(BF16)

                @pl.when(at_end)
                def _():
                    hop(zs.at[ph, near_h, k], ph, near_h, k, inner).start()

    def near_sums(ph):
        @pl.when(jnp.logical_not(at_end))
        def _():
            for k in range(K):
                hop(zs.at[ph, near_h, k], ph, near_h, k, inner).wait_recv()
                zt[ph, near_h, k] = (
                    zs[ph, near_h, k].astype(F32) + zr[ph, near_h, k].astype(F32)
                ).astype(BF16)
                hop(zt.at[ph, near_h, k], ph, near_h, k, inner).start()

    def far_sums(ph):
        for k in range(K):
            hop(zs.at[ph, far_h, k], ph, far_h, k, outer).wait_recv()
            total = (zs[ph, far_h, k].astype(F32) + zr[ph, far_h, k].astype(F32)).astype(BF16)

            @pl.when(at_end)
            def _():
                fg[ph][k, :, pl.ds(pl.multiple_of(far_h * half, half), half), :] = total
                back(ph, far_h, k, inner).start()

            @pl.when(jnp.logical_not(at_end))
            def _():
                zt[ph, far_h, k] = total
                hop(zt.at[ph, far_h, k], ph, far_h, k, outer).start()

    def far_back(ph):
        @pl.when(jnp.logical_not(at_end))
        def _():
            for k in range(K):
                back(ph, far_h, k, inner).wait_recv()
                back(ph, far_h, k, inner).start()

    def near_back(ph):
        for k in range(K):
            back(ph, near_h, k, outer).wait_recv()

            @pl.when(jnp.logical_not(at_end))
            def _():
                back(ph, near_h, k, outer).start()

    def drain(ph):
        for k in range(K):
            hop(zs.at[ph, near_h, k], ph, near_h, k, inner).wait_send()
            back(ph, far_h, k, inner).wait_send()

        @pl.when(jnp.logical_not(at_end))
        def _():
            for k in range(K):
                hop(zt.at[ph, far_h, k], ph, far_h, k, outer).wait_send()
                back(ph, near_h, k, outer).wait_send()

    grad_two = (cot[...].astype(F32) * slope(pre_two[...].astype(F32))).astype(BF16).astype(F32)
    stage_grad(0, grad_two)
    pl.semaphore_wait(barrier, len(partners))
    g_sent = send_grad(0)
    wide_one = pre_one[...].astype(F32)
    stage_feat(0, (wide_one * jax.nn.sigmoid(wide_one)).reshape(p, HX, C))
    a_sent = send_feat(0)
    stage_feat(1, inputs[...].astype(F32).reshape(p, HX, C))
    build_weights(filt_two)
    gx[:, 0] = jnp.zeros((R, X, 3 * C), BF16)
    gx[:, H + 1] = jnp.zeros((R, X, 3 * C), BF16)
    arrive(relay_grad(0, g_sent))
    build_gx(0)
    data_terms(0)
    a_passed = relay_feat(0, a_sent)
    p_sent = merge_terms(0)
    i_sent = send_feat(1)
    arrive(a_passed)
    build_lhs(0)
    filt_terms(0)

    delta = part_sum(0, p_sent).reshape(p, H, X, C)
    grad_one = (delta * slope(pre_one[...].astype(F32))).astype(BF16).astype(F32)
    stage_grad(1, grad_one)
    g_sent = send_grad(1)
    build_weights(filt_one)
    i_passed = relay_feat(1, i_sent)
    near_sums(0)
    arrive(i_passed)
    build_lhs(1)
    g_passed = relay_grad(1, g_sent)
    far_sums(0)
    arrive(g_passed)
    build_gx(1)
    filt_terms(1)
    far_back(0)
    near_sums(1)
    data_terms(1)
    near_back(0)
    p_sent = merge_terms(1)
    far_sums(1)
    far_back(1)
    out_in[...] = part_sum(1, p_sent).astype(BF16).reshape(p, H, X, C)
    near_back(1)
    for c in pending:
        c.wait_send()
    drain(0)
    drain(1)


def solution(mesh):
    n, m = mesh.shape["rot"], mesh.shape["az"]

    def shards(inputs, pre_one, pre_two, cot, filt_one, filt_two):
        p, H, X, C = inputs.shape
        R, HX, K, nc = n * p, H * X, 3 * p, n // 2
        scale = float(R * H * X * m) ** -0.5
        dma = pltpu.SemaphoreType.DMA
        vmem = pl.BlockSpec(memory_space=pltpu.VMEM)
        sums = jax.ShapeDtypeStruct((K, 3, C, C), BF16)
        got, sum_one, sum_two = pl.pallas_call(
            functools.partial(kernel, n, m, p, H, X, C),
            out_shape=(jax.ShapeDtypeStruct((p, H, X, C), BF16), sums, sums),
            in_specs=[vmem] * 6,
            out_specs=(vmem,) * 3,
            scratch_shapes=[
                pltpu.VMEM((2, p, H, X, C), BF16),
                pltpu.VMEM((2, 2, p * H, C), BF16),
                pltpu.VMEM((2, p, C, HX), BF16),
                pltpu.VMEM((2, n, p, H, X, C), BF16),
                pltpu.VMEM((2, n, 2, p * H, C), BF16),
                pltpu.VMEM((2, n, p, C, HX), BF16),
                pltpu.VMEM((p * C, 9 * C), BF16),
                pltpu.VMEM((R, H + 2, X, 3 * C), BF16),
                pltpu.VMEM((3 * C, (R + p - 1) * HX), BF16),
                pltpu.VMEM((R, HX, p * C), F32),
                pltpu.VMEM((2, n, p, HX, C), BF16),
                pltpu.VMEM((2, nc, p, HX, C), BF16),
                pltpu.VMEM((2, nc, p, HX, C), BF16),
                pltpu.VMEM((2, nc, p, HX, C), BF16),
                pltpu.VMEM((2, 2, K, 3, C // 2, C), BF16),
                pltpu.VMEM((2, 2, K, 3, C // 2, C), BF16),
                pltpu.VMEM((2, 2, K, 3, C // 2, C), BF16),
            ]
            + [dma((2, nc))] * 4
            + [dma((2, 2, nc))] * 2
            + [dma((2, nc))] * 2
            + [dma((2, nc))] * 8
            + [dma((2, 2, K))] * 4,
            compiler_params=pltpu.CompilerParams(
                collective_id=0, has_side_effects=True, vmem_limit_bytes=60 * 1024 * 1024
            ),
        )(inputs, pre_one, pre_two, cot, filt_one, filt_two)

        def widen(v):
            return (v.astype(F32) * scale).reshape(p, 3, 3, C, C)

        return got, widen(sum_one), widen(sum_two)

    cells = P("rot", None, "az", None)
    banks = P("rot", None, None, None, None)
    return jax.shard_map(
        shards, mesh=mesh,
        in_specs=(cells,) * 4 + (banks,) * 2,
        out_specs=(cells, banks, banks),
        check_vma=False,
    )
```

time: 93.2 us -> 78 us (0.84); the launches traced: 92 us -> 77.8 us
  Pallas kernels: 86.4 us -> 73.6 us
  local copies, waits for them, and re-layouts: 4.97 us -> 0.63 us
  other arithmetic: 0 us -> 2.96 us
    pallas_call x1, Pallas kernels: 86.4 us -> 73.6 us  [shards(): pl.pallas_call(functools.partial(kernel, n, m, p, H, X, C), out_shape=(ja...]
    unnamed x5 -> x3, local copies, waits for them, and re-layouts: 4.97 us -> 0.63 us
    mul x0 -> x1, other arithmetic: none -> 2.96 us  [widen(): return (v.astype(F32) * scale).reshape(p, 3, 3, C, C)]
where the time goes in v2:
time: 78 us; the launch traced here: 77.8 us
  Pallas kernels  73.6 us (94%)
  other arithmetic  2.96 us (4%)
    pallas_call x1, Pallas kernels, shards(): pl.pallas_call(functools.partial(kernel, n, m, p, H, X, C), out_shape=(ja...  73.6 us
    mul x1, other arithmetic, widen(): return (v.astype(F32) * scale).reshape(p, 3, 3, C, C)  2.96 us

profile of v2, /device:TPU:0, one launch (start us, length us, event | category | flops | bytes accessed | tf_op | source)
XLA Modules:
  0.0 77.8 jit_solution(10760964280785806313)
XLA Ops:
  0.6 73.6 %shard_map.85 = (bf16[2,4,32,128]{3,2,1,0:T(8,128)(2,1)}, bf16[6,3,128,128]{3,2,1,0:T(8,128)(2,1)}, bf16[6,3,128,128]{3,2,1,0:T(8,128)(2,1)}) custom-call(bf16[2,4,32,128]{3,2,1,0:T(8,128)(2,1)} %inputs.1, bf16[2,4,32,128]{3,2,1,0:T(8,128)(2,1)} %pre_one.1, bf16[2,4,32,128]{3,2,1,0:T(8,128)(2,1)} %pre_two.1, bf16[2,4,32,128]{3,2,1,0:T(8,128)(2,1)} %cot.1, ...), custom_call_target="tpu_custom_call" | custom-call | tf_op jit(solution)/shard_map/pallas_call | solution.py:385
  74.2 0.0 copy-start
  74.2 3.0 %convert_multiply_fusion = (f32[6,3,128,128]{3,2,1,0:T(8,128)}, f32[6,3,128,128]{3,2,1,0:T(8,128)}) fusion(bf16[6,3,128,128]{3,2,1,0:T(8,128)(2,1)} %get-tuple-element.8, bf16[6,3,128,128]{3,2,1,0:T(8,128)(2,1)} %get-tuple-element.7), kind=kLoop, calls=%fused_computation | loop fusion | flops 1179648 | bytes 3538944 | tf_op jit(solution)/shard_map/mul | solution.py:420
  77.2 0.0 copy-done
  77.2 0.6 copy.10
Async XLA Ops:
  74.2 3.0 %copy-start = (bf16[2,4,32,128]{3,2,1,0:T(8,128)(2,1)S(1)}, bf16[2,4,32,128]{3,2,1,0:T(8,128)(2,1)}, u32[]{:S(2)}) copy-start(bf16[2,4,32,128]{3,2,1,0:T(8,128)(2,1)} %get-tuple-element.14) | copy-start | bytes 196612

commit v3 on v2

--- a/solution.py
+++ b/solution.py
@@ -28,8 +28,7 @@
     R = n * p
     HX = H * X
     nc = n // 2
-    half = C // 2
-    K = 3 * p
+    K = 9 * p
     me = lax.axis_index("rot")
     z = lax.axis_index("az")
     core = lax.rem(me, 2)
@@ -239,21 +238,21 @@
     fg = (out_f2, out_f1)
     lower = z < m // 2
     near_pos = jnp.where(lower, z, m - 1 - z)
-    near_h = jnp.where(lower, 0, 1)
-    far_h = 1 - near_h
     right, left = jnp.minimum(z + 1, m - 1), jnp.maximum(z - 1, 0)
     inner = jnp.where(lower, right, left)
     outer = jnp.where(lower, left, right)
     at_end = near_pos == 0
-
-    def final(ph, h, k):
-        return fg[ph].at[k, :, pl.ds(pl.multiple_of(h * half, half), half), :]
-
-    def hop(src, ph, h, k, az):
-        return copy(src, zr.at[ph, h, k], z_ss.at[ph, h, k], z_rs.at[ph, h, k], me, az)
-
-    def back(ph, h, k, az):
-        return copy(final(ph, h, k), final(ph, h, k), y_ss.at[ph, h, k], y_rs.at[ph, h, k], me, az)
+    at_mid = near_pos == m // 2 - 1
+    slot = jnp.where(at_mid, 1, 0)
+
+    def inward(src, ph, k):
+        return copy(src, zr.at[ph, slot, k], z_ss.at[ph, k], z_rs.at[ph, slot, k], me, inner)
+
+    def crossed_in(ph, w, k):
+        return copy(zr.at[ph, w, k], zr.at[ph, w, k], z_ss.at[ph, k], z_rs.at[ph, w, k], me, inner)
+
+    def outward(ph, k):
+        return copy(fg[ph].at[k], fg[ph].at[k], y_ss.at[ph, k], y_rs.at[ph, k], me, outer)
 
     def filt_terms(ph):
         right_side = gx[:, 1 : H + 1].reshape(R * HX, 3 * C)
@@ -262,65 +261,48 @@
                 lhs[:, s * HX : (s + R) * HX], right_side, preferred_element_type=F32
             )
             for i in range(3):
-                k = s * 3 + i
                 for j in range(3):
-                    tile = got[i * C : (i + 1) * C, j * C : (j + 1) * C]
-                    zs[ph, :, k, j] = tile.reshape(2, half, C).astype(BF16)
-
-                @pl.when(at_end)
-                def _():
-                    hop(zs.at[ph, near_h, k], ph, near_h, k, inner).start()
-
-    def near_sums(ph):
+                    zs[ph, (s * 3 + i) * 3 + j] = got[i * C : (i + 1) * C, j * C : (j + 1) * C].astype(BF16)
+
+            @pl.when(at_end)
+            def _():
+                for k in range(s * 9, s * 9 + 9):
+                    inward(zs.at[ph, k], ph, k).start()
+
+    def go_in(ph, a, b):
+        @pl.when(jnp.logical_not(at_end))
+        def _():
+            for k in range(K * a // 18, K * b // 18):
+                crossed_in(ph, 0, k).wait_recv()
+                zt[ph, k] = (zs[ph, k].astype(F32) + zr[ph, 0, k].astype(F32)).astype(BF16)
+                inward(zt.at[ph, k], ph, k).start()
+
+    base = zs if m == 2 else zt
+
+    def go_out(ph, a, b):
+        for k in range(K * a // 18, K * b // 18):
+
+            @pl.when(at_mid)
+            def _():
+                crossed_in(ph, 1, k).wait_recv()
+                fg[ph][k] = (base[ph, k].astype(F32) + zr[ph, 1, k].astype(F32)).astype(BF16)
+
+            @pl.when(jnp.logical_not(at_mid))
+            def _():
+                outward(ph, k).wait_recv()
+
+            @pl.when(jnp.logical_not(at_end))
+            def _():
+                outward(ph, k).start()
+
+    def drain(ph):
+        for k in range(K):
+            crossed_in(ph, 0, k).wait_send()
+
         @pl.when(jnp.logical_not(at_end))
         def _():
             for k in range(K):
-                hop(zs.at[ph, near_h, k], ph, near_h, k, inner).wait_recv()
-                zt[ph, near_h, k] = (
-                    zs[ph, near_h, k].astype(F32) + zr[ph, near_h, k].astype(F32)
-                ).astype(BF16)
-                hop(zt.at[ph, near_h, k], ph, near_h, k, inner).start()
-
-    def far_sums(ph):
-        for k in range(K):
-            hop(zs.at[ph, far_h, k], ph, far_h, k, outer).wait_recv()
-            total = (zs[ph, far_h, k].astype(F32) + zr[ph, far_h, k].astype(F32)).astype(BF16)
-
-            @pl.when(at_end)
-            def _():
-                fg[ph][k, :, pl.ds(pl.multiple_of(far_h * half, half), half), :] = total
-                back(ph, far_h, k, inner).start()
-
-            @pl.when(jnp.logical_not(at_end))
-            def _():
-                zt[ph, far_h, k] = total
-                hop(zt.at[ph, far_h, k], ph, far_h, k, outer).start()
-
-    def far_back(ph):
-        @pl.when(jnp.logical_not(at_end))
-        def _():
-            for k in range(K):
-                back(ph, far_h, k, inner).wait_recv()
-                back(ph, far_h, k, inner).start()
-
-    def near_back(ph):
-        for k in range(K):
-            back(ph, near_h, k, outer).wait_recv()
-
-            @pl.when(jnp.logical_not(at_end))
-            def _():
-                back(ph, near_h, k, outer).start()
-
-    def drain(ph):
-        for k in range(K):
-            hop(zs.at[ph, near_h, k], ph, near_h, k, inner).wait_send()
-            back(ph, far_h, k, inner).wait_send()
-
-        @pl.when(jnp.logical_not(at_end))
-        def _():
-            for k in range(K):
-                hop(zt.at[ph, far_h, k], ph, far_h, k, outer).wait_send()
-                back(ph, near_h, k, outer).wait_send()
+                outward(ph, k).wait_send()
 
     grad_two = (cot[...].astype(F32) * slope(pre_two[...].astype(F32))).astype(BF16).astype(F32)
     stage_grad(0, grad_two)
@@ -347,25 +329,32 @@
     grad_one = (delta * slope(pre_one[...].astype(F32))).astype(BF16).astype(F32)
     stage_grad(1, grad_one)
     g_sent = send_grad(1)
+    i_passed = relay_feat(1, i_sent)
+    go_in(0, 0, 2)
     build_weights(filt_one)
-    i_passed = relay_feat(1, i_sent)
-    near_sums(0)
     arrive(i_passed)
     build_lhs(1)
+    go_in(0, 2, 6)
     g_passed = relay_grad(1, g_sent)
-    far_sums(0)
+    go_in(0, 6, 9)
+    go_out(0, 0, 3)
     arrive(g_passed)
     build_gx(1)
+    go_in(0, 9, 12)
+    go_out(0, 3, 7)
     filt_terms(1)
-    far_back(0)
-    near_sums(1)
+    go_in(0, 12, 16)
+    go_out(0, 7, 12)
     data_terms(1)
-    near_back(0)
+    go_in(0, 16, 18)
     p_sent = merge_terms(1)
-    far_sums(1)
-    far_back(1)
+    go_out(0, 12, 18)
+    go_in(1, 0, 4)
     out_in[...] = part_sum(1, p_sent).astype(BF16).reshape(p, H, X, C)
-    near_back(1)
+    for k in range(4, 18):
+        go_in(1, k, k + 1)
+        go_out(1, k - 4, k - 3)
+    go_out(1, 14, 18)
     for c in pending:
         c.wait_send()
     drain(0)
@@ -377,11 +366,11 @@
 
     def shards(inputs, pre_one, pre_two, cot, filt_one, filt_two):
         p, H, X, C = inputs.shape
-        R, HX, K, nc = n * p, H * X, 3 * p, n // 2
+        R, HX, K, nc = n * p, H * X, 9 * p, n // 2
         scale = float(R * H * X * m) ** -0.5
         dma = pltpu.SemaphoreType.DMA
         vmem = pl.BlockSpec(memory_space=pltpu.VMEM)
-        sums = jax.ShapeDtypeStruct((K, 3, C, C), BF16)
+        sums = jax.ShapeDtypeStruct((K, C, C), BF16)
         got, sum_one, sum_two = pl.pallas_call(
             functools.partial(kernel, n, m, p, H, X, C),
             out_shape=(jax.ShapeDtypeStruct((p, H, X, C), BF16), sums, sums),
@@ -402,15 +391,15 @@
                 pltpu.VMEM((2, nc, p, HX, C), BF16),
                 pltpu.VMEM((2, nc, p, HX, C), BF16),
                 pltpu.VMEM((2, nc, p, HX, C), BF16),
-                pltpu.VMEM((2, 2, K, 3, C // 2, C), BF16),
-                pltpu.VMEM((2, 2, K, 3, C // 2, C), BF16),
-                pltpu.VMEM((2, 2, K, 3, C // 2, C), BF16),
+                pltpu.VMEM((2, K, C, C), BF16),
+                pltpu.VMEM((2, 2, K, C, C), BF16),
+                pltpu.VMEM((2, K, C, C), BF16),
             ]
             + [dma((2, nc))] * 4
             + [dma((2, 2, nc))] * 2
             + [dma((2, nc))] * 2
             + [dma((2, nc))] * 8
-            + [dma((2, 2, K))] * 4,
+            + [dma((2, K)), dma((2, 2, K)), dma((2, K)), dma((2, K))],
             compiler_params=pltpu.CompilerParams(
                 collective_id=0, has_side_effects=True, vmem_limit_bytes=60 * 1024 * 1024
             ),

time: 78 us -> 71.6 us (0.918)
  Pallas kernels: 73.6 us -> 67.2 us
    pallas_call x1, Pallas kernels: 73.6 us -> 67.2 us  [shards(): pl.pallas_call(functools.partial(kernel, n, m, p, H, X, C), out_shape=(ja...]
where the time goes in v3:
time: 71.6 us; the launch traced here: 71.4 us
  Pallas kernels  67.2 us (94%)
  other arithmetic  2.96 us (4%)
    pallas_call x1, Pallas kernels, shards(): pl.pallas_call(functools.partial(kernel, n, m, p, H, X, C), out_shape=(ja...  67.2 us
    mul x1, other arithmetic, widen(): return (v.astype(F32) * scale).reshape(p, 3, 3, C, C)  2.96 us

profile of v3, /device:TPU:0, one launch (start us, length us, event | category | flops | bytes accessed | tf_op | source)
XLA Modules:
  0.0 71.4 jit_solution(11443073466174610633)
XLA Ops:
  0.6 67.2 %shard_map.85 = (bf16[2,4,32,128]{3,2,1,0:T(8,128)(2,1)}, bf16[18,128,128]{2,1,0:T(8,128)(2,1)}, bf16[18,128,128]{2,1,0:T(8,128)(2,1)}) custom-call(bf16[2,4,32,128]{3,2,1,0:T(8,128)(2,1)} %inputs.1, bf16[2,4,32,128]{3,2,1,0:T(8,128)(2,1)} %pre_one.1, bf16[2,4,32,128]{3,2,1,0:T(8,128)(2,1)} %pre_two.1, bf16[2,4,32,128]{3,2,1,0:T(8,128)(2,1)} %cot.1, ...), custom_call_target="tpu_custom_call" | custom-call | tf_op jit(solution)/shard_map/pallas_call | solution.py:374
  67.8 0.0 copy-start
  67.8 3.0 %convert_multiply_fusion = (f32[18,128,128]{2,1,0:T(8,128)}, f32[18,128,128]{2,1,0:T(8,128)}) fusion(bf16[18,128,128]{2,1,0:T(8,128)(2,1)} %get-tuple-element.8, bf16[18,128,128]{2,1,0:T(8,128)(2,1)} %get-tuple-element.7), kind=kLoop, calls=%fused_computation | loop fusion | flops 1179648 | bytes 3538944 | tf_op jit(solution)/shard_map/mul | solution.py:409
  70.8 0.0 copy-done
  70.8 0.6 copy.10
Async XLA Ops:
  67.8 3.0 %copy-start = (bf16[2,4,32,128]{3,2,1,0:T(8,128)(2,1)S(1)}, bf16[2,4,32,128]{3,2,1,0:T(8,128)(2,1)}, u32[]{:S(2)}) copy-start(bf16[2,4,32,128]{3,2,1,0:T(8,128)(2,1)} %get-tuple-element.14) | copy-start | bytes 196612

commit v4 on v3

--- a/solution.py
+++ b/solution.py
@@ -264,10 +264,14 @@
                 for j in range(3):
                     zs[ph, (s * 3 + i) * 3 + j] = got[i * C : (i + 1) * C, j * C : (j + 1) * C].astype(BF16)
 
-            @pl.when(at_end)
-            def _():
-                for k in range(s * 9, s * 9 + 9):
-                    inward(zs.at[ph, k], ph, k).start()
+            if ph == 1:
+                begin(ph, s * 18 // p, (s + 1) * 18 // p)
+
+    def begin(ph, a, b):
+        @pl.when(at_end)
+        def _():
+            for k in range(K * a // 18, K * b // 18):
+                inward(zs.at[ph, k], ph, k).start()
 
     def go_in(ph, a, b):
         @pl.when(jnp.logical_not(at_end))
@@ -324,11 +328,13 @@
     arrive(a_passed)
     build_lhs(0)
     filt_terms(0)
+    begin(0, 0, 6)
 
     delta = part_sum(0, p_sent).reshape(p, H, X, C)
     grad_one = (delta * slope(pre_one[...].astype(F32))).astype(BF16).astype(F32)
     stage_grad(1, grad_one)
     g_sent = send_grad(1)
+    begin(0, 6, 18)
     i_passed = relay_feat(1, i_sent)
     go_in(0, 0, 2)
     build_weights(filt_one)

time: 71.6 us -> 65.8 us (0.919)
  Pallas kernels: 67.2 us -> 61.4 us
    pallas_call x1, Pallas kernels: 67.2 us -> 61.4 us  [shards(): pl.pallas_call(functools.partial(kernel, n, m, p, H, X, C), out_shape=(ja...]
where the time goes in v4:
time: 65.8 us; the launch traced here: 65.7 us
  Pallas kernels  61.4 us (93%)
  other arithmetic  2.96 us (4%)
    pallas_call x1, Pallas kernels, shards(): pl.pallas_call(functools.partial(kernel, n, m, p, H, X, C), out_shape=(ja...  61.4 us
    mul x1, other arithmetic, widen(): return (v.astype(F32) * scale).reshape(p, 3, 3, C, C)  2.96 us

profile of v4, /device:TPU:0, one launch (start us, length us, event | category | flops | bytes accessed | tf_op | source)
XLA Modules:
  0.0 65.7 jit_solution(17255144214107877661)
XLA Ops:
  0.6 61.4 %shard_map.85 = (bf16[2,4,32,128]{3,2,1,0:T(8,128)(2,1)}, bf16[18,128,128]{2,1,0:T(8,128)(2,1)}, bf16[18,128,128]{2,1,0:T(8,128)(2,1)}) custom-call(bf16[2,4,32,128]{3,2,1,0:T(8,128)(2,1)} %inputs.1, bf16[2,4,32,128]{3,2,1,0:T(8,128)(2,1)} %pre_one.1, bf16[2,4,32,128]{3,2,1,0:T(8,128)(2,1)} %pre_two.1, bf16[2,4,32,128]{3,2,1,0:T(8,128)(2,1)} %cot.1, ...), custom_call_target="tpu_custom_call" | custom-call | tf_op jit(solution)/shard_map/pallas_call | solution.py:380
  62.1 0.0 copy-start
  62.1 3.0 %convert_multiply_fusion = (f32[18,128,128]{2,1,0:T(8,128)}, f32[18,128,128]{2,1,0:T(8,128)}) fusion(bf16[18,128,128]{2,1,0:T(8,128)(2,1)} %get-tuple-element.8, bf16[18,128,128]{2,1,0:T(8,128)(2,1)} %get-tuple-element.7), kind=kLoop, calls=%fused_computation | loop fusion | flops 1179648 | bytes 3538944 | tf_op jit(solution)/shard_map/mul | solution.py:415
  65.0 0.0 copy-done
  65.0 0.6 copy.10
Async XLA Ops:
  62.1 3.0 %copy-start = (bf16[2,4,32,128]{3,2,1,0:T(8,128)(2,1)S(1)}, bf16[2,4,32,128]{3,2,1,0:T(8,128)(2,1)}, u32[]{:S(2)}) copy-start(bf16[2,4,32,128]{3,2,1,0:T(8,128)(2,1)} %get-tuple-element.14) | copy-start | bytes 196612
